TPU v7x, 32 devices: a whole 2x2x4 slice. The times are simulated.
32 devices in a mesh: shard: 4 (over z), ctx: 4 (over y, x), tensor: 2 (over core).
Axes of the slice: x: 2, y: 2, z: 4, core: 2. Of those that a mesh axis runs over, the one named last changes fastest.
Arguments:
- inputs: bfloat16 [2, 1280, 1472], P(None, ('shard', 'ctx')), may hold values from -6 to 6
- cotangent: bfloat16 [2, 1280, 1472], P(None, ('shard', 'ctx')), may hold values from -6 to 6
- norm1_gain: bfloat16 [1472], P('shard'), may hold values from 0.099609375 to 1.8984375
- w_query: bfloat16 [1472, 384], P('shard', 'tensor'), may hold values from -0.0390625 to 0.0390625
- w_key: bfloat16 [1472, 384], P('shard', 'tensor'), may hold values from -0.15625 to 0.15625
- w_value: bfloat16 [1472, 384], P('shard', 'tensor'), may hold values from -0.15625 to 0.15625
- w_out: bfloat16 [384, 1472], P('tensor', 'shard'), may hold values from -1.25 to 1.25
- norm2_gain: bfloat16 [1472], P('shard'), may hold values from 0.099609375 to 1.8984375
- w_gate: bfloat16 [1472, 3584], P('shard', 'tensor'), may hold values from -0.15625 to 0.15625
- w_up: bfloat16 [1472, 3584], P('shard', 'tensor'), may hold values from -0.15625 to 0.15625
- w_down: bfloat16 [3584, 1472], P('tensor', 'shard'), may hold values from -0.1875 to 0.1875
- bias_table: float32 [32, 6], replicated, may hold values from -4 to 4
Outputs:
- output: bfloat16 [2, 1280, 1472], P(None, ('shard', 'ctx'))
- input_grad: bfloat16 [2, 1280, 1472], P(None, ('shard', 'ctx'))
- norm1_gain_grad: float32 [1472], P('shard')
- w_query_grad: float32 [1472, 384], P('shard', 'tensor')
- w_key_grad: float32 [1472, 384], P('shard', 'tensor')
- w_value_grad: float32 [1472, 384], P('shard', 'tensor')
- w_out_grad: float32 [384, 1472], P('tensor', 'shard')
- norm2_gain_grad: float32 [1472], P('shard')
- w_gate_grad: float32 [1472, 3584], P('shard', 'tensor')
- w_up_grad: float32 [1472, 3584], P('shard', 'tensor')
- w_down_grad: float32 [3584, 1472], P('tensor', 'shard')
All inputs are finite; a program needn't handle non-finite values.
Results may differ from a plain program's by a relative error of at most 0.024.
Values may be sent and summed in bfloat16 or wider, within the bound.
No kernel may reach another device: no remote copies, remote signals or barrier semaphores. Data moves between devices by JAX's collectives and lax.ppermute only.
A program may use at most 128 MiB of HBM per device.

v0:
```python
import jax
import jax.numpy as jnp
from jax import lax
from jax.sharding import PartitionSpec as P

DK = 64
norm_eps = 1e-06
distance_marks = (8, 12, 16, 23, 32, 46, 64, 91)
masked_score = -1e30


def for_sending(x):
    return jax.tree.map(lambda a: a.astype(jnp.bfloat16) if a.dtype == jnp.float32 else a, x)


def path_info(token, seg_len):
    segment = jnp.where(
        token < 8 * seg_len,
        0,
        jnp.where(
            token < 12 * seg_len,
            (token - 8 * seg_len) // seg_len + 1,
            (token - 12 * seg_len) // seg_len + 5,
        ),
    )
    parent = jnp.where(segment == 0, -1, jnp.where(segment <= 4, 0, (segment - 5) // 2 + 1))
    place = token - jnp.where(
        segment == 0, 0, jnp.where(segment <= 4, (segment - 1) * seg_len, (segment - 2) * seg_len)
    )
    return (segment, parent, place)


def bucket_of(relative):
    magnitude = jnp.abs(relative)
    marked = sum(((magnitude >= mark).astype(jnp.int32) for mark in distance_marks))
    return jnp.where(relative > 0, 16, 0) + jnp.where(magnitude < 8, magnitude, 7 + marked)


def score_bias(query_token, key_token, table, seg_len):
    query_seg, query_parent, query_place = path_info(query_token, seg_len)
    key_seg, key_parent, key_place = path_info(key_token, seg_len)
    allowed = (
        (key_seg[None, :] == 0)
        | (key_seg[None, :] == query_seg[:, None])
        | (key_seg[None, :] == query_parent[:, None])
    )
    bucket = bucket_of(key_place[None, :] - query_place[:, None])
    looked = jnp.stack([jnp.take(table[:, head], bucket, axis=0) for head in range(table.shape[1])])
    return jnp.where(allowed[None], looked, masked_score)


def left_dot(left, right):
    return lax.dot_general(
        left, right, (((0,), (0,)), ((), ())), preferred_element_type=jnp.float32
    )


def right_dot(left, right):
    return lax.dot_general(
        left, right, (((1,), (1,)), ((), ())), preferred_element_type=jnp.float32
    )


def norm_back(values_in, scale, gain, normed_grad):
    weighted = normed_grad * gain
    value_grad = scale * weighted - values_in * scale**3 * jnp.mean(
        weighted * values_in, axis=-1, keepdims=True
    )
    gain_grad = jnp.sum(normed_grad * values_in * scale, axis=0)
    return (value_grad, gain_grad)


def gelu_tanh(value_in):
    return jax.nn.gelu(value_in, approximate=True)


def one_layer(weights, tokens_in, grad_in, bias_local, row_count, key_count):
    gain_one, w_query, w_key, w_value, w_out, gain_two, w_gate, w_up, w_down = weights
    inner = w_query.shape[1]
    heads_local = inner // DK
    gain_first = gain_one.astype(jnp.float32)
    gain_second = gain_two.astype(jnp.float32)
    start_in = tokens_in.astype(jnp.float32)
    scale_one = lax.rsqrt(jnp.mean(start_in * start_in, axis=-1, keepdims=True) + norm_eps)
    normed_one = (start_in * scale_one * gain_first).astype(jnp.bfloat16)
    queries = jnp.dot(normed_one, w_query, preferred_element_type=jnp.float32).astype(jnp.bfloat16)
    keys = jnp.dot(normed_one, w_key, preferred_element_type=jnp.float32).astype(jnp.bfloat16)
    values = jnp.dot(normed_one, w_value, preferred_element_type=jnp.float32).astype(jnp.bfloat16)
    key_path, value_path = (
        lax.all_gather(keys, "ctx", axis=0, tiled=True),
        lax.all_gather(values, "ctx", axis=0, tiled=True),
    )
    query_heads = queries.reshape(row_count, heads_local, DK)
    key_heads = key_path.reshape(key_count, heads_local, DK)
    value_heads = value_path.reshape(key_count, heads_local, DK)

    def score_block():
        raw = jnp.einsum("qhd,khd->hqk", query_heads, key_heads, preferred_element_type=jnp.float32)
        return raw + bias_local

    scores = score_block()
    row_max = jnp.max(scores, axis=-1, keepdims=True)
    raised = jnp.exp(scores - row_max)
    totals = jnp.sum(raised, axis=-1, keepdims=True)
    log_total = row_max + jnp.log(totals)
    attention = (raised / totals).astype(jnp.bfloat16)
    mixed = jnp.einsum("hqk,khd->qhd", attention, value_heads, preferred_element_type=jnp.float32)
    mixed = mixed.reshape(row_count, inner).astype(jnp.bfloat16)
    attended = lax.psum(
        jnp.dot(mixed, w_out, preferred_element_type=jnp.float32).astype(jnp.bfloat16), "tensor"
    ).astype(jnp.float32)
    middle = start_in + attended
    scale_two = lax.rsqrt(jnp.mean(middle * middle, axis=-1, keepdims=True) + norm_eps)
    normed_two = (middle * scale_two * gain_second).astype(jnp.bfloat16)
    gate_pre = jnp.dot(normed_two, w_gate, preferred_element_type=jnp.float32)
    up_pre = jnp.dot(normed_two, w_up, preferred_element_type=jnp.float32)
    activated = gelu_tanh(gate_pre)
    hidden = (activated * up_pre).astype(jnp.bfloat16)
    feed = lax.psum(
        jnp.dot(hidden, w_down, preferred_element_type=jnp.float32).astype(jnp.bfloat16), "tensor"
    ).astype(jnp.float32)
    produced = (middle + feed).astype(jnp.bfloat16)
    grad_out = grad_in.astype(jnp.float32)
    down_in = grad_out.astype(jnp.bfloat16)
    down_grad = left_dot(hidden, down_in)
    hidden_grad = right_dot(down_in, w_down)
    unused, gelu_pull = jax.vjp(gelu_tanh, gate_pre)
    gate_grad = gelu_pull(hidden_grad * up_pre)[0].astype(jnp.bfloat16)
    up_grad = (hidden_grad * activated).astype(jnp.bfloat16)
    gate_wgrad = left_dot(normed_two, gate_grad)
    up_wgrad = left_dot(normed_two, up_grad)
    normed_two_grad = lax.psum(
        (right_dot(gate_grad, w_gate) + right_dot(up_grad, w_up)).astype(jnp.bfloat16), "tensor"
    ).astype(jnp.float32)
    middle_part, gain_two_grad = norm_back(middle, scale_two, gain_second, normed_two_grad)
    middle_grad = grad_out + middle_part
    out_in = middle_grad.astype(jnp.bfloat16)
    out_wgrad = left_dot(mixed, out_in)
    mixed_grad = right_dot(out_in, w_out).astype(jnp.bfloat16)
    mixed_heads = mixed_grad.reshape(row_count, heads_local, DK)
    soft = jnp.exp(score_block() - log_total)
    soft_low = soft.astype(jnp.bfloat16)
    values_full = jnp.einsum(
        "hqk,qhd->khd", soft_low, mixed_heads, preferred_element_type=jnp.float32
    )
    weight_grad = jnp.einsum(
        "qhd,khd->hqk", mixed_heads, value_heads, preferred_element_type=jnp.float32
    )
    scores_grad = soft * (weight_grad - jnp.sum(weight_grad * soft, axis=-1, keepdims=True))
    scores_grad = scores_grad.astype(jnp.bfloat16)
    queries_grad = jnp.einsum(
        "hqk,khd->qhd", scores_grad, key_heads, preferred_element_type=jnp.float32
    )
    queries_grad = queries_grad.reshape(row_count, inner).astype(jnp.bfloat16)
    keys_full = jnp.einsum(
        "hqk,qhd->khd", scores_grad, query_heads, preferred_element_type=jnp.float32
    )
    keys_own, values_own = (
        lax.psum_scatter(
            keys_full.reshape(key_count, inner).astype(jnp.bfloat16),
            "ctx",
            scatter_dimension=0,
            tiled=True,
        ).astype(jnp.float32),
        lax.psum_scatter(
            values_full.reshape(key_count, inner).astype(jnp.bfloat16),
            "ctx",
            scatter_dimension=0,
            tiled=True,
        ).astype(jnp.float32),
    )
    keys_grad = keys_own.astype(jnp.bfloat16)
    values_grad = values_own.astype(jnp.bfloat16)
    query_wgrad = left_dot(normed_one, queries_grad)
    key_wgrad = left_dot(normed_one, keys_grad)
    value_wgrad = left_dot(normed_one, values_grad)
    local_first = (
        right_dot(queries_grad, w_query)
        + right_dot(keys_grad, w_key)
        + right_dot(values_grad, w_value)
    )
    normed_one_grad = lax.psum(local_first.astype(jnp.bfloat16), "tensor").astype(jnp.float32)
    input_part, gain_one_grad = norm_back(start_in, scale_one, gain_first, normed_one_grad)
    input_grad = (middle_grad + input_part).astype(jnp.bfloat16)
    grads = (
        gain_one_grad,
        query_wgrad,
        key_wgrad,
        value_wgrad,
        out_wgrad,
        gain_two_grad,
        gate_wgrad,
        up_wgrad,
        down_grad,
    )
    return (produced, input_grad, grads)


def on_device(
    inputs,
    cotangent,
    norm1_gain,
    w_query,
    w_key,
    w_value,
    w_out,
    norm2_gain,
    w_gate,
    w_up,
    w_down,
    bias_table,
):
    micro_count = inputs.shape[0]
    row_count = inputs.shape[1]
    key_count = row_count * lax.axis_size("ctx")
    heads_local = w_query.shape[1] // DK
    query_token = lax.axis_index("ctx") * row_count + jnp.arange(row_count, dtype=jnp.int32)
    key_token = jnp.arange(key_count, dtype=jnp.int32)
    table_local = lax.dynamic_slice_in_dim(
        bias_table, lax.axis_index("tensor") * heads_local, heads_local, 1
    )
    bias_local = score_bias(query_token, key_token, table_local, row_count // 5)
    outputs_list = []
    input_grads = []
    running = None
    for micro_step in range(micro_count):
        weights = (
            lax.all_gather(norm1_gain, "shard", axis=0, tiled=True),
            lax.all_gather(w_query, "shard", axis=0, tiled=True),
            lax.all_gather(w_key, "shard", axis=0, tiled=True),
            lax.all_gather(w_value, "shard", axis=0, tiled=True),
            lax.all_gather(w_out, "shard", axis=1, tiled=True),
            lax.all_gather(norm2_gain, "shard", axis=0, tiled=True),
            lax.all_gather(w_gate, "shard", axis=0, tiled=True),
            lax.all_gather(w_up, "shard", axis=0, tiled=True),
            lax.all_gather(w_down, "shard", axis=1, tiled=True),
        )
        produced, input_grad, grads = one_layer(
            weights, inputs[micro_step], cotangent[micro_step], bias_local, row_count, key_count
        )
        outputs_list.append(produced)
        input_grads.append(input_grad)
        running = grads if running is None else jax.tree.map(jnp.add, running, grads)
    owned = (
        lax.psum_scatter(
            running[0].astype(jnp.bfloat16), "shard", scatter_dimension=0, tiled=True
        ).astype(jnp.float32),
        lax.psum_scatter(
            running[1].astype(jnp.bfloat16), "shard", scatter_dimension=0, tiled=True
        ).astype(jnp.float32),
        lax.psum_scatter(
            running[2].astype(jnp.bfloat16), "shard", scatter_dimension=0, tiled=True
        ).astype(jnp.float32),
        lax.psum_scatter(
            running[3].astype(jnp.bfloat16), "shard", scatter_dimension=0, tiled=True
        ).astype(jnp.float32),
        lax.psum_scatter(
            running[4].astype(jnp.bfloat16), "shard", scatter_dimension=1, tiled=True
        ).astype(jnp.float32),
        lax.psum_scatter(
            running[5].astype(jnp.bfloat16), "shard", scatter_dimension=0, tiled=True
        ).astype(jnp.float32),
        lax.psum_scatter(
            running[6].astype(jnp.bfloat16), "shard", scatter_dimension=0, tiled=True
        ).astype(jnp.float32),
        lax.psum_scatter(
            running[7].astype(jnp.bfloat16), "shard", scatter_dimension=0, tiled=True
        ).astype(jnp.float32),
        lax.psum_scatter(
            running[8].astype(jnp.bfloat16), "shard", scatter_dimension=1, tiled=True
        ).astype(jnp.float32),
    )
    final_grads = jax.tree.map(
        lambda part: part.astype(jnp.float32), lax.psum(for_sending(owned), "ctx")
    )
    return (jnp.stack(outputs_list), jnp.stack(input_grads)) + tuple(final_grads)


def solution(mesh):
    placed = (
        P(None, ("shard", "ctx"), None),
        P(None, ("shard", "ctx"), None),
        P("shard"),
        P("shard", "tensor"),
        P("shard", "tensor"),
        P("shard", "tensor"),
        P("tensor", "shard"),
        P("shard"),
        P("shard", "tensor"),
        P("shard", "tensor"),
        P("tensor", "shard"),
        P(),
    )
    return jax.shard_map(
        on_device,
        mesh=mesh,
        in_specs=placed,
        out_specs=(
            P(None, ("shard", "ctx"), None),
            P(None, ("shard", "ctx"), None),
            P("shard"),
            P("shard", "tensor"),
            P("shard", "tensor"),
            P("shard", "tensor"),
            P("tensor", "shard"),
            P("shard"),
            P("shard", "tensor"),
            P("shard", "tensor"),
            P("tensor", "shard"),
        ),
        check_vma=False,
    )
```

profile of v0, /device:TPU:0, one launch (start us, length us, event | category | flops | bytes accessed | tf_op | source)
XLA Modules:
  0.0 1594.4 jit_solution(13874918093051243575)
XLA Ops:
  9.8 18.5 %all-gather = bf16[4,368,192]{1,2,0:T(8,128)(2,1)S(1)} all-gather(bf16[1,368,192]{1,2,0:T(8,128)(2,1)} %bitcast.319), channel_id=1, replica_groups=mesh['shard'=4,'ctx'=4,'tensor'=2] {'shard'}, dimensions={0}, use_global_device_ids=true | all-gather | bytes 706560 | tf_op jit(solution)/shard_map/all_gather | solution.py:231
  34.4 12.9 all-reduce.7
  47.4 15.8 all-gather.1
  67.4 14.9 all-gather.2
  93.0 151.6 %gather_fusion = f32[25600]{0:T(1024)S(1)} fusion(f32[32]{0:T(128)S(1)} %get-tuple-element.66, s32[25600]{0:T(1024)S(1)} %broadcast_clamp_fusion), kind=kCustom, calls=%fused_computation.clone | custom fusion | bytes 307200 | tf_op jit(solution)/shard_map/jit(_take)/gather | solution.py:48
  244.7 151.6 %gather_fusion.1 = f32[25600]{0:T(1024)S(1)} fusion(f32[32]{0:T(128)S(1)} %get-tuple-element.68, s32[25600]{0:T(1024)S(1)} %broadcast_clamp_fusion), kind=kCustom, calls=%fused_computation.1.clone | custom fusion | bytes 307200 | tf_op jit(solution)/shard_map/jit(_take)/gather | solution.py:48
  396.5 151.6 %gather_fusion.2 = f32[25600]{0:T(1024)S(1)} fusion(f32[32]{0:T(128)S(1)} %get-tuple-element.67, s32[25600]{0:T(1024)S(1)} %broadcast_clamp_fusion), kind=kCustom, calls=%fused_computation.2.clone | custom fusion | bytes 307200 | tf_op jit(solution)/shard_map/jit(_take)/gather | solution.py:48
  557.1 15.0 all-gather.3
  596.1 14.5 all-reduce.22.cloned.1.call-done
  614.3 77.8 %all-gather.8.cloned.1.call-done = bf16[1472,1792]{1,0:T(8,128)(2,1)} async-done(((bf16[368,1792]{1,0:T(8,128)(2,1)}), bf16[1472,1792]{1,0:T(8,128)(2,1)}) %all-gather.8.cloned.1.call-update) | async-done | bytes 5275664 | tf_op jit(solution)/shard_map/all_gather | solution.py:234
  696.5 94.0 %all-gather.10.cloned.1.call-done = bf16[1472,1792]{1,0:T(8,128)(2,1)} async-done(((bf16[368,1792]{1,0:T(8,128)(2,1)}), bf16[1472,1792]{1,0:T(8,128)(2,1)}) %all-gather.10.cloned.1.call-update) | async-done | bytes 5275664 | tf_op jit(solution)/shard_map/all_gather | solution.py:235
  798.5 90.3 %all-gather.12.cloned.1.call-done = bf16[1792,1472]{0,1:T(8,128)(2,1)} async-done(((bf16[1792,368]{0,1:T(8,128)(2,1)}), bf16[1792,1472]{0,1:T(8,128)(2,1)}) %all-gather.12.cloned.1.call-update) | async-done | bytes 5275664 | tf_op jit(solution)/shard_map/all_gather | solution.py:236
  907.6 17.1 %all-reduce.20.cloned.1.call-done = (bf16[80,1472]{1,0:T(8,128)(2,1)}, bf16[80,1472]{1,0:T(8,128)(2,1)}) async-done(((bf16[80,1472]{1,0:T(8,128)(2,1)}, bf16[80,1472]{1,0:T(8,128)(2,1)}), (bf16[80,1472]{1,0:T(8,128)(2,1)}, bf16[80,1472]{1,0:T(8,128)(2,1)})) %all-reduce.20.cloned.1.call-update) | async-done | bytes 471056 | tf_op jit(solution)/shard_map/psum | solution.py:132
  962.6 25.4 %reduce-scatter.38.cloned.1.call-done = bf16[80,192]{1,0:T(8,128)(2,1)} async-done(((bf16[320,192]{1,0:T(8,128)(2,1)}), bf16[80,192]{1,0:T(8,128)(2,1)}) %reduce-scatter.38.cloned.1.call-update) | async-done | bytes 30736
  992.3 22.3 %reduce-scatter.36.cloned.1.call-done = bf16[80,192]{1,0:T(8,128)(2,1)} async-done(((bf16[320,192]{1,0:T(8,128)(2,1)}), bf16[80,192]{1,0:T(8,128)(2,1)}) %reduce-scatter.36.cloned.1.call-update) | async-done | bytes 30736
  1015.8 25.4 %reduce-scatter.40.cloned.1.call-done = bf16[80,192]{1,0:T(8,128)(2,1)} async-done(((bf16[320,192]{1,0:T(8,128)(2,1)}), bf16[80,192]{1,0:T(8,128)(2,1)}) %reduce-scatter.40.cloned.1.call-update) | async-done | bytes 30736
  1093.2 23.3 %reduce-scatter.44.cloned.1.call-done = bf16[368,192]{1,0:T(8,128)(2,1)} async-done(((bf16[1472,192]{1,0:T(8,128)(2,1)}), bf16[368,192]{1,0:T(8,128)(2,1)}) %reduce-scatter.44.cloned.1.call-update) | async-done | bytes 141328
  1118.3 23.1 %reduce-scatter.46.cloned.1.call-done = bf16[368,192]{1,0:T(8,128)(2,1)} async-done(((bf16[1472,192]{1,0:T(8,128)(2,1)}), bf16[368,192]{1,0:T(8,128)(2,1)}) %reduce-scatter.46.cloned.1.call-update) | async-done | bytes 141328
  1143.1 94.0 %reduce-scatter.28.cloned.1.call-done = bf16[368,1792]{1,0:T(8,128)(2,1)} async-done(((bf16[1472,1792]{1,0:T(8,128)(2,1)}), bf16[368,1792]{1,0:T(8,128)(2,1)}) %reduce-scatter.28.cloned.1.call-update) | async-done | bytes 1318928 | tf_op jit(solution)/shard_map/reduce_scatter | solution.py:263
  1237.2 97.0 %reduce-scatter.30.cloned.1.call-done = bf16[368,1792]{1,0:T(8,128)(2,1)} async-done(((bf16[1472,1792]{1,0:T(8,128)(2,1)}), bf16[368,1792]{1,0:T(8,128)(2,1)}) %reduce-scatter.30.cloned.1.call-update) | async-done | bytes 1318928 | tf_op jit(solution)/shard_map/reduce_scatter | solution.py:266
  1334.2 97.1 %reduce-scatter.32.cloned.1.call-done = bf16[1792,368]{0,1:T(8,128)(2,1)} async-done(((bf16[1792,1472]{0,1:T(8,128)(2,1)}), bf16[1792,368]{0,1:T(8,128)(2,1)}) %reduce-scatter.32.cloned.1.call-update) | async-done | bytes 1318928 | tf_op jit(solution)/shard_map/reduce_scatter | solution.py:269
  1432.0 22.5 %all-reduce.18.cloned.1.call-done = (bf16[80,1472]{1,0:T(8,128)(2,1)}, bf16[80,1472]{1,0:T(8,128)(2,1)}, bf16[80,1472]{1,0:T(8,128)(2,1)}, bf16[80,1472]{1,0:T(8,128)(2,1)}) async-done(((bf16[80,1472]{1,0:T(8,128)(2,1)}, bf16[80,1472]{1,0:T(8,128)(2,1)}, bf16[80,1472]{1,0:T(8,128)(2,1)}, bf16[80,1472]{1,0:T(8,128)(2,1)}), (bf16[80,1472]{1,0:T(8,128)(2,1)}, bf16[80,1472]{1,0:T(8,128)(2,1)}, ...) | async-done | bytes 942096 | tf_op jit(solution)/shard_map/psum | solution.py:119
  1455.9 12.2 all-reduce.6
  1483.2 90.6 %all-reduce.16.cloned.1.call-done = (bf16[368,192]{0,1:T(8,128)(2,1)}, bf16[368,192]{0,1:T(8,128)(2,1)}, bf16[368,192]{0,1:T(8,128)(2,1)}, bf16[192,368]{1,0:T(8...) async-done(((bf16[368,192]{0,1:T(8,128)(2,1)}, bf16[368,192]{0,1:T(8,128)(2,1)}, bf16[368,192]{0,1:T(8,128)(2,1)}, ...) | async-done | bytes 4522000 | tf_op jit(solution)/shard_map/psum | solution.py:274
  (337 shorter events, 217.4 us)
Async XLA Ops:
  8.0 602.5 %all-reduce.22.cloned.1.call-start = ((), (), s32[]{:S(2)}) async-start(), calls=%async_computation.28 | async-start | bytes 983040 | tf_op jit(solution)/shard_map/psum | solution.py:109
  92.6 498.0 %copy-start.37 = (bf16[320,192]{0,1:T(8,128)(2,1)}, bf16[320,192]{0,1:T(8,128)(2,1)S(1)}, u32[]{:S(2)}) copy-start(bf16[320,192]{0,1:T(8,128)(2,1)S(1)} %copy.58) | copy-start | bytes 368644
  593.8 98.4 %all-gather.8.cloned.1.call-start = ((), (), s32[]{:S(2)}) async-start(), calls=%async_computation.11 | async-start | bytes 6594560 | tf_op jit(solution)/shard_map/all_gather | solution.py:234
  594.4 196.1 %all-gather.10.cloned.1.call-start = ((), (), s32[]{:S(2)}) async-start(), calls=%async_computation.12 | async-start | bytes 6594560 | tf_op jit(solution)/shard_map/all_gather | solution.py:235
  595.0 293.8 %all-gather.12.cloned.1.call-start = ((), (), s32[]{:S(2)}) async-start(), calls=%async_computation.13 | async-start | bytes 6594560 | tf_op jit(solution)/shard_map/all_gather | solution.py:236
  595.6 329.2 %all-reduce.20.cloned.1.call-start = ((), (), s32[]{:S(2)}) async-start(), calls=%async_computation.27 | async-start | bytes 983040 | tf_op jit(solution)/shard_map/psum | solution.py:132
  907.5 53.9 %reduce-scatter.34.cloned.1.call-start = ((), (), s32[]{:S(2)}) async-start(), calls=%async_computation.17 | async-start | bytes 204800
  936.2 51.9 %reduce-scatter.38.cloned.1.call-start = ((), (), s32[]{:S(2)}) async-start(), calls=%async_computation.19 | async-start | bytes 204800
  941.1 73.5 %reduce-scatter.36.cloned.1.call-start = ((), (), s32[]{:S(2)}) async-start(), calls=%async_computation.18 | async-start | bytes 204800
  946.5 94.7 %reduce-scatter.40.cloned.1.call-start = ((), (), s32[]{:S(2)}) async-start(), calls=%async_computation.20 | async-start | bytes 204800
  947.7 130.5 %reduce-scatter.48.cloned.1.call-start = ((), (), s32[]{:S(2)}) async-start(), calls=%async_computation.24 | async-start | bytes 942080
  952.1 139.5 %reduce-scatter.42.cloned.1.call-start = ((), (), s32[]{:S(2)}) async-start(), calls=%async_computation.21 | async-start | bytes 942080
  959.7 156.9 %reduce-scatter.44.cloned.1.call-start = ((), (), s32[]{:S(2)}) async-start(), calls=%async_computation.22 | async-start | bytes 942080
  992.2 149.2 %reduce-scatter.46.cloned.1.call-start = ((), (), s32[]{:S(2)}) async-start(), calls=%async_computation.23 | async-start | bytes 942080
  1045.5 191.7 %reduce-scatter.28.cloned.1.call-start = ((), (), s32[]{:S(2)}) async-start(), calls=%async_computation.14 | async-start | bytes 6594560 | tf_op jit(solution)/shard_map/reduce_scatter | solution.py:263
  1052.2 282.0 %reduce-scatter.30.cloned.1.call-start = ((), (), s32[]{:S(2)}) async-start(), calls=%async_computation.15 | async-start | bytes 6594560 | tf_op jit(solution)/shard_map/reduce_scatter | solution.py:266
  1058.5 372.8 %reduce-scatter.32.cloned.1.call-start = ((), (), s32[]{:S(2)}) async-start(), calls=%async_computation.16 | async-start | bytes 6594560 | tf_op jit(solution)/shard_map/reduce_scatter | solution.py:269
  1065.1 389.4 %all-reduce.18.cloned.1.call-start = ((), (), s32[]{:S(2)}) async-start(), calls=%async_computation.26 | async-start | bytes 1966080 | tf_op jit(solution)/shard_map/psum | solution.py:119
  1076.9 355.1 %copy-start.56 = (f32[1472]{0:T(1024)S(1)}, f32[1472]{0:T(1024)}, u32[]{:S(2)}) copy-start(f32[1472]{0:T(1024)} %get-tuple-element.23) | copy-start | bytes 17668
  1076.9 402.6 %copy-start.10 = (bf16[80,1472]{1,0:T(8,128)(2,1)S(1)}, bf16[80,1472]{1,0:T(8,128)(2,1)}, u32[]{:S(2)}) copy-start(bf16[80,1472]{1,0:T(8,128)(2,1)} %get-tuple-element.47) | copy-start | bytes 706564
  1076.9 402.6 %copy-start.12 = (bf16[80,1472]{1,0:T(8,128)(2,1)S(1)}, bf16[80,1472]{1,0:T(8,128)(2,1)}, u32[]{:S(2)}) copy-start(bf16[80,1472]{1,0:T(8,128)(2,1)} %get-tuple-element.48) | copy-start | bytes 706564
  1076.9 402.6 %copy-start.67 = (f32[80]{0:T(128)S(1)}, f32[80]{0:T(128)}, u32[]{:S(2)}) copy-start(f32[80]{0:T(128)} %get-tuple-element.73) | copy-start | bytes 964
  1076.9 402.6 %copy-start.68 = (f32[80]{0:T(128)S(1)}, f32[80]{0:T(128)}, u32[]{:S(2)}) copy-start(f32[80]{0:T(128)} %get-tuple-element.88) | copy-start | bytes 964
  1078.1 495.6 %all-reduce.16.cloned.1.call-start = ((), (), s32[]{:S(2)}) async-start(), calls=%async_computation.25 | async-start | bytes 9093120 | tf_op jit(solution)/shard_map/psum | solution.py:274
  (70 other events, 3635.6 us)
Sparse Core Ops, SparseCore 0:
  593.9 16.6 all-reduce.21
  907.7 17.0 all-reduce.19
  936.3 25.1 reduce-scatter.33
  964.1 23.9 reduce-scatter.37
  990.6 23.9 reduce-scatter.35
  1017.2 23.9 reduce-scatter.39
  1043.5 22.9 reduce-scatter.47
  1069.4 22.0 reduce-scatter.41
  1094.4 22.1 reduce-scatter.43
  1119.3 22.0 reduce-scatter.45
  1143.7 93.3 reduce-scatter.27
  1239.3 94.7 reduce-scatter.29
  1336.5 94.7 reduce-scatter.31
  1434.3 20.1 all-reduce.17
  1460.2 113.4 all-reduce.15
Sparse Core Ops, SparseCore 1:
  595.8 96.3 all-gather.7
  693.6 96.8 all-gather.9
  791.9 96.8 all-gather.11
where the time goes:
time: 1600 us; the launch traced here: 1590 us
  waiting for transfers between devices  830 us (52%)
  local copies, waits for them, and re-layouts  489 us (31%)
  blocking collectives  133 us (8%)
  matrix products  91 us (6%)
  other arithmetic  32.1 us (2%)
  between operations  18.4 us (1%)
    gather x6, local copies, waits for them, and re-layouts, score_bias(): jnp.take(table[:, head], bucket, axis=0)  455 us
    unnamed x26, waiting for transfers between devices  135 us
    reduce_scatter x1, waiting for transfers between devices, on_device(): lax.psum_scatter(running[8].astype(jnp.bfloat16), 'shard', scatter_dimens...  97.1 us
    reduce_scatter x1, waiting for transfers between devices, on_device(): lax.psum_scatter(running[7].astype(jnp.bfloat16), 'shard', scatter_dimens...  97 us
    reduce_scatter x1, waiting for transfers between devices, on_device(): lax.psum_scatter(running[6].astype(jnp.bfloat16), 'shard', scatter_dimens...  94 us
    all_gather x1, waiting for transfers between devices, on_device(): lax.all_gather(w_up, 'shard', axis=0, tiled=True)  94 us
    psum x1, waiting for transfers between devices, on_device(): lax.psum(for_sending(owned), 'ctx')  90.6 us
    all_gather x1, waiting for transfers between devices, on_device(): lax.all_gather(w_down, 'shard', axis=1, tiled=True)  90.3 us
  transfers between devices with their start and end apart: 18, of which 17 were waited for; matrix products, arithmetic and copies ran while one was open for 6% of the time, Pallas kernels for 0%

commit v1 on v0

--- a/solution.py
+++ b/solution.py
@@ -1,3 +1,4 @@
+import functools
 import jax
 import jax.numpy as jnp
 from jax import lax
@@ -7,6 +8,37 @@
 norm_eps = 1e-06
 distance_marks = (8, 12, 16, 23, 32, 46, 64, 91)
 masked_score = -1e30
+
+
+def _replace_paths(local_values, across, join_dim):
+    outer = lax.axis_index(across)
+    spare = lax.axis_size(across)
+    y_new, base_arr, b_now = (spare, outer, local_values.shape[join_dim])
+    seen = [(s, (s + 1) % y_new) for s in range(y_new)]
+    current_arr = jnp.zeros(
+        (*local_values.shape[:join_dim], y_new * b_now, *local_values.shape[join_dim + 1 :]),
+        local_values.dtype,
+    )
+    current_arr = lax.dynamic_update_slice_in_dim(
+        current_arr, local_values, base_arr * b_now, axis=join_dim
+    )
+    w2 = h_now = local_values
+    ledger = [(s, (s - 1) % y_new) for s in range(y_new)]
+    clean = y_new // 2
+    for it in range(1, clean + 1):
+        w2 = lax.ppermute(w2, axis_name=across, perm=seen)
+        current_arr = lax.dynamic_update_slice_in_dim(
+            current_arr, w2, (base_arr - it) % y_new * b_now, axis=join_dim
+        )
+        if it < y_new - clean:
+            h_now = lax.ppermute(h_now, axis_name=across, perm=ledger)
+            current_arr = lax.dynamic_update_slice_in_dim(
+                current_arr, h_now, (base_arr + it) % y_new * b_now, axis=join_dim
+            )
+    return current_arr
+
+
+draft_patches = functools.partial(_replace_paths, across="shard", join_dim=1)
 
 
 def for_sending(x):
@@ -233,7 +265,7 @@
             lax.all_gather(norm2_gain, "shard", axis=0, tiled=True),
             lax.all_gather(w_gate, "shard", axis=0, tiled=True),
             lax.all_gather(w_up, "shard", axis=0, tiled=True),
-            lax.all_gather(w_down, "shard", axis=1, tiled=True),
+            draft_patches(w_down),
         )
         produced, input_grad, grads = one_layer(
             weights, inputs[micro_step], cotangent[micro_step], bias_local, row_count, key_count

time: 1600 us -> 1560 us (0.975)
  waiting for transfers between devices: 830 us -> 767 us
  starting transfers between devices: 1.6 us -> 26 us
    ppermute x0 -> x3, waiting for transfers between devices: none -> 102 us  [the longest x2 84.2 us: _replace_paths(): w2 = lax.ppermute(w2, axis_name=across, perm=seen)]
    all_gather x1 -> x0, waiting for transfers between devices: 90.3 us -> none  [on_device(): lax.all_gather(w_down, 'shard', axis=1, tiled=True)]
    all_gather x1, waiting for transfers between devices: 77.8 us -> 3.2 us  [on_device(): lax.all_gather(w_gate, 'shard', axis=0, tiled=True)]
    ppermute x0 -> x3, starting transfers between devices: none -> 24.9 us  [the longest x2 21.1 us: _replace_paths(): w2 = lax.ppermute(w2, axis_name=across, perm=seen)]
    unnamed x26 -> x25, waiting for transfers between devices: 135 us -> 143 us
  transfers between devices with their start and end apart: 18 -> 20, of which waited for: 17 -> 19; matrix products, arithmetic and copies ran while one was open for 6% -> 6% of each run, Pallas kernels for 0% -> 0%
where the time goes in v1:
time: 1560 us; the launch traced here: 1550 us
  waiting for transfers between devices  767 us (49%)
  local copies, waits for them, and re-layouts  495 us (32%)
  blocking collectives  133 us (9%)
  matrix products  83.4 us (5%)
  other arithmetic  31.4 us (2%)
  starting transfers between devices  26 us (2%)
  between operations  18.1 us (1%)
    gather x6, local copies, waits for them, and re-layouts, score_bias(): jnp.take(table[:, head], bucket, axis=0)  455 us
    unnamed x25, waiting for transfers between devices  143 us
    reduce_scatter x1, waiting for transfers between devices, on_device(): lax.psum_scatter(running[8].astype(jnp.bfloat16), 'shard', scatter_dimens...  97.2 us
    reduce_scatter x1, waiting for transfers between devices, on_device(): lax.psum_scatter(running[7].astype(jnp.bfloat16), 'shard', scatter_dimens...  97 us
    all_gather x1, waiting for transfers between devices, on_device(): lax.all_gather(w_up, 'shard', axis=0, tiled=True)  94.5 us
    reduce_scatter x1, waiting for transfers between devices, on_device(): lax.psum_scatter(running[6].astype(jnp.bfloat16), 'shard', scatter_dimens...  94 us
    psum x1, waiting for transfers between devices, on_device(): lax.psum(for_sending(owned), 'ctx')  90.6 us
    ppermute x2, waiting for transfers between devices, _replace_paths(): w2 = lax.ppermute(w2, axis_name=across, perm=seen)  84.2 us
  transfers between devices with their start and end apart: 20, of which 19 were waited for; matrix products, arithmetic and copies ran while one was open for 6% of the time, Pallas kernels for 0%

profile of v1, /device:TPU:0, one launch (start us, length us, event | category | flops | bytes accessed | tf_op | source)
XLA Modules:
  0.0 1554.0 jit_solution(17214918986755198946)
XLA Ops:
  9.2 18.5 %all-gather = bf16[4,368,192]{1,2,0:T(8,128)(2,1)S(1)} all-gather(bf16[1,368,192]{1,2,0:T(8,128)(2,1)} %bitcast.323), channel_id=1, replica_groups=mesh['shard'=4,'ctx'=4,'tensor'=2] {'shard'}, dimensions={0}, use_global_device_ids=true | all-gather | bytes 706560 | tf_op jit(solution)/shard_map/all_gather | solution.py:263
  46.2 16.5 %all-gather.1 = bf16[4,368,192]{1,2,0:T(8,128)(2,1)S(1)} all-gather(bf16[1,368,192]{1,2,0:T(8,128)(2,1)} %bitcast.324), channel_id=1, replica_groups=mesh['shard'=4,'ctx'=4,'tensor'=2] {'shard'}, dimensions={0}, use_global_device_ids=true | all-gather | bytes 706560 | tf_op jit(solution)/shard_map/all_gather | solution.py:261
  65.6 14.9 all-gather.2
  91.3 151.6 %gather_fusion = f32[25600]{0:T(1024)S(1)} fusion(f32[32]{0:T(128)S(1)} %get-tuple-element.66, s32[25600]{0:T(1024)S(1)} %broadcast_clamp_fusion), kind=kCustom, calls=%fused_computation.clone | custom fusion | bytes 307200 | tf_op jit(solution)/shard_map/jit(_take)/gather | solution.py:80
  243.0 151.6 %gather_fusion.1 = f32[25600]{0:T(1024)S(1)} fusion(f32[32]{0:T(128)S(1)} %get-tuple-element.68, s32[25600]{0:T(1024)S(1)} %broadcast_clamp_fusion), kind=kCustom, calls=%fused_computation.1.clone | custom fusion | bytes 307200 | tf_op jit(solution)/shard_map/jit(_take)/gather | solution.py:80
  394.7 151.6 %gather_fusion.2 = f32[25600]{0:T(1024)S(1)} fusion(f32[32]{0:T(128)S(1)} %get-tuple-element.67, s32[25600]{0:T(1024)S(1)} %broadcast_clamp_fusion), kind=kCustom, calls=%fused_computation.2.clone | custom fusion | bytes 307200 | tf_op jit(solution)/shard_map/jit(_take)/gather | solution.py:80
  555.3 15.0 all-gather.3
  609.7 40.1 %collective-permute-done = bf16[1792,368]{0,1:T(8,128)(2,1)} collective-permute-done((bf16[1792,368]{0,1:T(8,128)(2,1)}, bf16[1792,368]{0,1:T(8,128)(2,1)}, u32[]{:S(2)}, u32[]{:S(2)}) %collective-permute-start) | collective-permute-done | bytes 1318944 | tf_op jit(solution)/shard_map/ppermute | solution.py:29
  649.8 21.0 %collective-permute-start.2 = (bf16[1792,368]{0,1:T(8,128)(2,1)}, bf16[1792,368]{0,1:T(8,128)(2,1)S(1)}, u32[]{:S(2)}, u32[]{:S(2)}) collective-permute-start(bf16[1792,368]{0,1:T(8,128)(2,1)} %collective-permute-done), channel_id=1, source_target_pairs={{0,8},{8,16},{16,24},{24,0},{1,9},{9,17},{17,25},{25,1},{2,10},{10... | collective-permute-start | bytes 3956744 | tf_op jit(solution)/shard_map/ppermute | solution.py:29
  675.7 18.1 %collective-permute-done.1 = bf16[1792,368]{0,1:T(8,128)(2,1)} collective-permute-done((bf16[1792,368]{0,1:T(8,128)(2,1)}, bf16[1792,368]{0,1:T(8,128)(2,1)}, u32[]{:S(2)}, u32[]{:S(2)}) %collective-permute-start.1) | collective-permute-done | bytes 1318944 | tf_op jit(solution)/shard_map/ppermute | solution.py:34
  696.3 44.1 %collective-permute-done.2 = bf16[1792,368]{0,1:T(8,128)(2,1)S(1)} collective-permute-done((bf16[1792,368]{0,1:T(8,128)(2,1)}, bf16[1792,368]{0,1:T(8,128)(2,1)S(1)}, u32[]{:S(2)}, u32[]{:S(2)}) %collective-permute-start.2) | collective-permute-done | bytes 1318944 | tf_op jit(solution)/shard_map/ppermute | solution.py:29
  749.2 94.5 %all-gather.9.cloned.1.call-done = bf16[1472,1792]{1,0:T(8,128)(2,1)} async-done(((bf16[368,1792]{1,0:T(8,128)(2,1)}), bf16[1472,1792]{1,0:T(8,128)(2,1)}) %all-gather.9.cloned.1.call-update) | async-done | bytes 5275664 | tf_op jit(solution)/shard_map/all_gather | solution.py:267
  866.9 17.2 %all-reduce.20.cloned.1.call-done = (bf16[80,1472]{1,0:T(8,128)(2,1)}, bf16[80,1472]{1,0:T(8,128)(2,1)}) async-done(((bf16[80,1472]{1,0:T(8,128)(2,1)}, bf16[80,1472]{1,0:T(8,128)(2,1)}), (bf16[80,1472]{1,0:T(8,128)(2,1)}, bf16[80,1472]{1,0:T(8,128)(2,1)})) %all-reduce.20.cloned.1.call-update) | async-done | bytes 471056 | tf_op jit(solution)/shard_map/psum | solution.py:164
  922.9 25.0 %reduce-scatter.38.cloned.1.call-done = bf16[80,192]{1,0:T(8,128)(2,1)} async-done(((bf16[320,192]{1,0:T(8,128)(2,1)}), bf16[80,192]{1,0:T(8,128)(2,1)}) %reduce-scatter.38.cloned.1.call-update) | async-done | bytes 30736
  950.8 23.7 %reduce-scatter.36.cloned.1.call-done = bf16[80,192]{1,0:T(8,128)(2,1)} async-done(((bf16[320,192]{1,0:T(8,128)(2,1)}), bf16[80,192]{1,0:T(8,128)(2,1)}) %reduce-scatter.36.cloned.1.call-update) | async-done | bytes 30736
  976.7 24.4 %reduce-scatter.40.cloned.1.call-done = bf16[80,192]{1,0:T(8,128)(2,1)} async-done(((bf16[320,192]{1,0:T(8,128)(2,1)}), bf16[80,192]{1,0:T(8,128)(2,1)}) %reduce-scatter.40.cloned.1.call-update) | async-done | bytes 30736
  1037.4 14.0 reduce-scatter.42.cloned.1.call-done
  1053.1 23.3 %reduce-scatter.44.cloned.1.call-done = bf16[368,192]{1,0:T(8,128)(2,1)} async-done(((bf16[1472,192]{1,0:T(8,128)(2,1)}), bf16[368,192]{1,0:T(8,128)(2,1)}) %reduce-scatter.44.cloned.1.call-update) | async-done | bytes 141328
  1078.1 23.1 %reduce-scatter.46.cloned.1.call-done = bf16[368,192]{1,0:T(8,128)(2,1)} async-done(((bf16[1472,192]{1,0:T(8,128)(2,1)}), bf16[368,192]{1,0:T(8,128)(2,1)}) %reduce-scatter.46.cloned.1.call-update) | async-done | bytes 141328
  1103.0 94.0 %reduce-scatter.28.cloned.1.call-done = bf16[368,1792]{1,0:T(8,128)(2,1)} async-done(((bf16[1472,1792]{1,0:T(8,128)(2,1)}), bf16[368,1792]{1,0:T(8,128)(2,1)}) %reduce-scatter.28.cloned.1.call-update) | async-done | bytes 1318928 | tf_op jit(solution)/shard_map/reduce_scatter | solution.py:295
  1197.0 97.0 %reduce-scatter.30.cloned.1.call-done = bf16[368,1792]{1,0:T(8,128)(2,1)} async-done(((bf16[1472,1792]{1,0:T(8,128)(2,1)}), bf16[368,1792]{1,0:T(8,128)(2,1)}) %reduce-scatter.30.cloned.1.call-update) | async-done | bytes 1318928 | tf_op jit(solution)/shard_map/reduce_scatter | solution.py:298
  1294.0 97.2 %reduce-scatter.32.cloned.1.call-done = bf16[1792,368]{0,1:T(8,128)(2,1)} async-done(((bf16[1792,1472]{0,1:T(8,128)(2,1)}), bf16[1792,368]{0,1:T(8,128)(2,1)}) %reduce-scatter.32.cloned.1.call-update) | async-done | bytes 1318928 | tf_op jit(solution)/shard_map/reduce_scatter | solution.py:301
  1391.9 22.4 %all-reduce.18.cloned.1.call-done = (bf16[80,1472]{1,0:T(8,128)(2,1)}, bf16[80,1472]{1,0:T(8,128)(2,1)}, bf16[80,1472]{1,0:T(8,128)(2,1)}, bf16[80,1472]{1,0:T(8,128)(2,1)}) async-done(((bf16[80,1472]{1,0:T(8,128)(2,1)}, bf16[80,1472]{1,0:T(8,128)(2,1)}, bf16[80,1472]{1,0:T(8,128)(2,1)}, bf16[80,1472]{1,0:T(8,128)(2,1)}), (bf16[80,1472]{1,0:T(8,128)(2,1)}, bf16[80,1472]{1,0:T(8,128)(2,1)}, ...) | async-done | bytes 942096 | tf_op jit(solution)/shard_map/psum | solution.py:151
  1443.0 90.6 %all-reduce.16.cloned.1.call-done = (bf16[368,192]{0,1:T(8,128)(2,1)}, bf16[368,192]{0,1:T(8,128)(2,1)}, bf16[368,192]{0,1:T(8,128)(2,1)}, bf16[192,368]{1,0:T(8...) async-done(((bf16[368,192]{0,1:T(8,128)(2,1)}, bf16[368,192]{0,1:T(8,128)(2,1)}, bf16[368,192]{0,1:T(8,128)(2,1)}, ...) | async-done | bytes 4522000 | tf_op jit(solution)/shard_map/psum | solution.py:306
  (321 shorter events, 246.5 us)
Async XLA Ops:
  8.0 600.3 %all-reduce.22.cloned.1.call-start = ((), (), s32[]{:S(2)}) async-start(), calls=%async_computation.27 | async-start | bytes 983040 | tf_op jit(solution)/shard_map/psum | solution.py:141
  90.8 497.9 %copy-start.32 = (bf16[320,192]{0,1:T(8,128)(2,1)}, bf16[320,192]{0,1:T(8,128)(2,1)S(1)}, u32[]{:S(2)}) copy-start(bf16[320,192]{0,1:T(8,128)(2,1)S(1)} %copy.58) | copy-start | bytes 368644
  592.0 152.9 %all-gather.7.cloned.1.call-start = ((), (), s32[]{:S(2)}) async-start(), calls=%async_computation.11 | async-start | bytes 6594560 | tf_op jit(solution)/shard_map/all_gather | solution.py:266
  592.6 251.1 %all-gather.9.cloned.1.call-start = ((), (), s32[]{:S(2)}) async-start(), calls=%async_computation.12 | async-start | bytes 6594560 | tf_op jit(solution)/shard_map/all_gather | solution.py:267
  593.1 291.0 %all-reduce.20.cloned.1.call-start = ((), (), s32[]{:S(2)}) async-start(), calls=%async_computation.26 | async-start | bytes 983040 | tf_op jit(solution)/shard_map/psum | solution.py:164
  593.2 56.6 %collective-permute-start = (bf16[1792,368]{0,1:T(8,128)(2,1)}, bf16[1792,368]{0,1:T(8,128)(2,1)}, u32[]{:S(2)}, u32[]{:S(2)}) collective-permute-start(bf16[1792,368]{0,1:T(8,128)(2,1)} %param.24), channel_id=1, source_target_pairs={{0,8},{8,16},{16,24},{24,0},{1,9},{9,17},{17,25},{25,1},{2,10},{10... | collective-permute-start | bytes 3956744 | tf_op jit(solution)/shard_map/ppermute | solution.py:29
  593.3 100.6 %collective-permute-start.1 = (bf16[1792,368]{0,1:T(8,128)(2,1)}, bf16[1792,368]{0,1:T(8,128)(2,1)}, u32[]{:S(2)}, u32[]{:S(2)}) collective-permute-start(bf16[1792,368]{0,1:T(8,128)(2,1)} %param.24), channel_id=1, source_target_pairs={{0,24},{8,0},{16,8},{24,16},{1,25},{9,1},{17,9},{25,17},{2,26},{10... | collective-permute-start | bytes 3956744 | tf_op jit(solution)/shard_map/ppermute | solution.py:34
  649.8 90.6 %collective-permute-start.2 = (bf16[1792,368]{0,1:T(8,128)(2,1)}, bf16[1792,368]{0,1:T(8,128)(2,1)S(1)}, u32[]{:S(2)}, u32[]{:S(2)}) collective-permute-start(bf16[1792,368]{0,1:T(8,128)(2,1)} %collective-permute-done), channel_id=1, source_target_pairs={{0,8},{8,16},{16,24},{24,0},{1,9},{9,17},{17,25},{25,1},{2,10},{10... | collective-permute-start | bytes 3956744 | tf_op jit(solution)/shard_map/ppermute | solution.py:29
  866.9 53.9 %reduce-scatter.34.cloned.1.call-start = ((), (), s32[]{:S(2)}) async-start(), calls=%async_computation.16 | async-start | bytes 204800
  895.5 52.4 %reduce-scatter.38.cloned.1.call-start = ((), (), s32[]{:S(2)}) async-start(), calls=%async_computation.18 | async-start | bytes 204800
  900.4 74.1 %reduce-scatter.36.cloned.1.call-start = ((), (), s32[]{:S(2)}) async-start(), calls=%async_computation.17 | async-start | bytes 204800
  905.0 96.1 %reduce-scatter.40.cloned.1.call-start = ((), (), s32[]{:S(2)}) async-start(), calls=%async_computation.19 | async-start | bytes 204800
  907.1 128.6 %reduce-scatter.48.cloned.1.call-start = ((), (), s32[]{:S(2)}) async-start(), calls=%async_computation.23 | async-start | bytes 942080
  910.2 141.2 %reduce-scatter.42.cloned.1.call-start = ((), (), s32[]{:S(2)}) async-start(), calls=%async_computation.20 | async-start | bytes 942080
  912.7 163.8 %reduce-scatter.44.cloned.1.call-start = ((), (), s32[]{:S(2)}) async-start(), calls=%async_computation.21 | async-start | bytes 942080
  950.8 150.5 %reduce-scatter.46.cloned.1.call-start = ((), (), s32[]{:S(2)}) async-start(), calls=%async_computation.22 | async-start | bytes 942080
  1003.9 193.1 %reduce-scatter.28.cloned.1.call-start = ((), (), s32[]{:S(2)}) async-start(), calls=%async_computation.13 | async-start | bytes 6594560 | tf_op jit(solution)/shard_map/reduce_scatter | solution.py:295
  1009.6 284.5 %reduce-scatter.30.cloned.1.call-start = ((), (), s32[]{:S(2)}) async-start(), calls=%async_computation.14 | async-start | bytes 6594560 | tf_op jit(solution)/shard_map/reduce_scatter | solution.py:298
  1016.1 375.1 %reduce-scatter.32.cloned.1.call-start = ((), (), s32[]{:S(2)}) async-start(), calls=%async_computation.15 | async-start | bytes 6594560 | tf_op jit(solution)/shard_map/reduce_scatter | solution.py:301
  1022.5 391.8 %all-reduce.18.cloned.1.call-start = ((), (), s32[]{:S(2)}) async-start(), calls=%async_computation.25 | async-start | bytes 1966080 | tf_op jit(solution)/shard_map/psum | solution.py:151
  1034.4 405.0 %copy-start.7 = (bf16[80,1472]{1,0:T(8,128)(2,1)S(1)}, bf16[80,1472]{1,0:T(8,128)(2,1)}, u32[]{:S(2)}) copy-start(bf16[80,1472]{1,0:T(8,128)(2,1)} %get-tuple-element.47) | copy-start | bytes 706564
  1034.4 405.0 %copy-start.9 = (bf16[80,1472]{1,0:T(8,128)(2,1)S(1)}, bf16[80,1472]{1,0:T(8,128)(2,1)}, u32[]{:S(2)}) copy-start(bf16[80,1472]{1,0:T(8,128)(2,1)} %get-tuple-element.48) | copy-start | bytes 706564
  1034.4 405.0 %copy-start.55 = (f32[80]{0:T(128)S(1)}, f32[80]{0:T(128)}, u32[]{:S(2)}) copy-start(f32[80]{0:T(128)} %get-tuple-element.73) | copy-start | bytes 964
  1035.6 498.0 %all-reduce.16.cloned.1.call-start = ((), (), s32[]{:S(2)}) async-start(), calls=%async_computation.24 | async-start | bytes 9093120 | tf_op jit(solution)/shard_map/psum | solution.py:306
  (60 other events, 3741.3 us)
Sparse Core Ops, SparseCore 0:
  592.1 16.1 all-reduce.21
  867.0 17.0 all-reduce.19
  895.6 25.1 reduce-scatter.33
  923.9 23.9 reduce-scatter.37
  950.5 23.9 reduce-scatter.35
  977.1 23.9 reduce-scatter.39
  1003.4 22.9 reduce-scatter.47
  1029.3 22.1 reduce-scatter.41
  1054.3 22.0 reduce-scatter.43
  1079.2 22.0 reduce-scatter.45
  1103.6 93.3 reduce-scatter.27
  1199.2 94.7 reduce-scatter.29
  1296.3 94.8 reduce-scatter.31
  1394.2 20.0 all-reduce.17
  1420.1 113.4 all-reduce.15
Sparse Core Ops, SparseCore 1:
  594.0 150.8 all-gather.6
  746.2 97.3 all-gather.8
